TPU v7x, 512 devices: a whole 4x4x16 slice. The times are simulated.
512 devices in a mesh: seq: 32 (over z, core), mp: 16 (over y, x).
Axes of the slice: x: 4, y: 4, z: 16, core: 2. Of those that a mesh axis runs over, the one named last changes fastest.
Arguments:
- continued_prompt_entries: bfloat16 [4096, 4096], P('seq', 'mp'), may hold values from -6 to 6
- padded_prompt_entries: bfloat16 [4096, 4096], P('seq', 'mp'), may hold values from -6 to 6
- prompt_live_extents: int32 [64], P('seq'), may hold values from 8 to 64, as said below
- preceding_entry_line: bfloat16 [4096], P('mp'), may hold values from -6 to 6
- carried_memory: float32 [64, 64, 64], P('mp'), may hold values from -24 to 24
- token_mixing_ratios: float32 [5, 4096], replicated, may hold values from 0.05 to 0.95
- acceptance_transform: bfloat16 [4096, 4096], P('seq', 'mp'), may hold values from -0.09375 to 0.09375
- lookup_transform: bfloat16 [4096, 4096], P('seq', 'mp'), may hold values from -0.09375 to 0.09375
- payload_transform: bfloat16 [4096, 4096], P('seq', 'mp'), may hold values from -0.09375 to 0.09375
- gating_transform: bfloat16 [4096, 4096], P('seq', 'mp'), may hold values from -0.09375 to 0.09375
- fading_baseline: float32 [4096], P('mp'), may hold values from -10 to -3.5
- fading_left_factor: bfloat16 [4096, 128], replicated, may hold values from -0.09375 to 0.09375
- fading_right_factor: bfloat16 [128, 4096], P(None, 'mp'), may hold values from -0.5 to 0.5
- present_reward: float32 [64, 64], P('mp'), may hold values from -3 to 3
- group_layer_scaling: float32 [4096], P('mp'), may hold values from 0.5 to 1.5
- group_layer_shift_term: float32 [4096], P('mp'), may hold values from -1.8 to 1.8
- final_transform: bfloat16 [4096, 4096], P('mp', 'seq'), may hold values from -0.09375 to 0.09375
Outputs:
- mixed: bfloat16 [32, 256, 4096], P('seq', 'mp')
- span_states: float32 [32, 64, 64, 64], P('seq', 'mp')
- request_states: float32 [64, 64, 64, 64], P('seq', 'mp')
Inputs may be any that keep to these rules, and one draw needn't show every extreme that they name: `prompt_live_extents`: some request has all 64 rows live.
All inputs are finite; a program needn't handle non-finite values.
Results may differ from a plain program's by a relative error of at most 0.0076.
Values may be sent and summed in bfloat16 or wider, within the bound.
A program may use at most 64 MiB of HBM per device.

v0:
```python
import jax
import jax.numpy as jnp
from jax import lax
from jax.sharding import PartitionSpec as P

BLK = 64
SEQ = ("z", "core")
norm_eps = 0.00064
highest = lax.Precision.HIGHEST


def seq_index():
    return lax.axis_index("z") * lax.axis_size("core") + lax.axis_index("core")


def seq_shift(x, by, length):
    pairs = [(i, i + by) for i in range(length) if i + by < length]
    return lax.ppermute(x, SEQ, pairs)


def exclusive_prefix(value, start, length):
    mine = seq_index()
    arrived = seq_shift(value, 1, length)
    total = jax.tree.map(lambda got, first: jnp.where(mine == 0, first, got), arrived, start)
    step = 1
    while step < length:
        got = seq_shift(total, step, length)
        joined = combine(got, total)
        total = jax.tree.map(lambda new, old: jnp.where(mine >= step, new, old), joined, total)
        step *= 2
    return total


def mix_rows(current, previous, weight):
    here = current.astype(jnp.float32)
    return (here + weight[None, :] * (previous.astype(jnp.float32) - here)).astype(jnp.bfloat16)


def block_sweep(
    evolving_memory,
    acceptance_entries,
    lookup_entries,
    payload_entries,
    log_fading_amount,
    diagonal_reward,
):
    inclusive = jnp.cumsum(log_fading_amount, axis=0)
    exclusive = inclusive - log_fading_amount
    recept_scaled = acceptance_entries * jnp.exp(exclusive)
    keys_scaled = lookup_entries * jnp.exp(-inclusive)
    scores = jnp.einsum("ihc,jhc->hij", recept_scaled, keys_scaled, precision=highest)
    count = acceptance_entries.shape[0]
    row_index = lax.broadcasted_iota(jnp.int32, (count, count), 0)
    col_index = lax.broadcasted_iota(jnp.int32, (count, count), 1)
    scores = jnp.where((row_index > col_index)[None], scores, 0.0)
    diagonal_contribution = jnp.sum(
        acceptance_entries * diagonal_reward[None] * lookup_entries, axis=-1, keepdims=True
    )
    answer_lines = (
        jnp.einsum("hij,jhd->ihd", scores, payload_entries, precision=highest)
        + diagonal_contribution * payload_entries
    )
    answer_lines = answer_lines + jnp.einsum(
        "ihc,hcd->ihd", recept_scaled, evolving_memory, precision=highest
    )
    total = inclusive[-1]
    carried = lookup_entries * jnp.exp(total[None] - inclusive)
    new_state = jnp.exp(total)[:, :, None] * evolving_memory + jnp.einsum(
        "jhc,jhd->hcd", carried, payload_entries, precision=highest
    )
    return (new_state, answer_lines)


def continued_recurrence(
    acceptance_entries, lookup_entries, payload_entries, log_fading_amount, diagonal_reward
):
    length, per_group_view, embedding_dimension = acceptance_entries.shape
    blocks = length // BLK

    def step(evolving_memory, entry_lines):
        return block_sweep(
            evolving_memory,
            entry_lines[0],
            entry_lines[1],
            entry_lines[2],
            entry_lines[3],
            diagonal_reward,
        )

    shaped = tuple(
        (
            a.reshape(blocks, BLK, per_group_view, embedding_dimension)
            for a in (acceptance_entries, lookup_entries, payload_entries, log_fading_amount)
        )
    )
    evolving_memory, results = lax.scan(
        step,
        jnp.zeros((per_group_view, embedding_dimension, embedding_dimension), jnp.float32),
        shaped,
    )
    return (evolving_memory, results.reshape(length, per_group_view, embedding_dimension))


def combine(earlier, later):
    return (earlier[0] + later[0], jnp.exp(later[0])[:, :, None] * earlier[1] + later[1])


def shifted_rows(current, edge_row, long_rows, requests, slot_rows):
    feature_part = current.shape[1]
    long_prev = jnp.concatenate([edge_row, current[: long_rows - 1]], axis=0)
    short_view = current[long_rows:].reshape(requests, slot_rows, feature_part)
    short_prev = jnp.concatenate(
        [jnp.zeros((requests, 1, feature_part), current.dtype), short_view[:, :-1]], axis=1
    )
    short_prev = short_prev.reshape(requests * slot_rows, feature_part)
    return jnp.concatenate([long_prev, short_prev], axis=0)


def on_device(
    continued_prompt_entries,
    padded_prompt_entries,
    prompt_live_extents,
    preceding_entry_line,
    carried_memory,
    token_mixing_ratios,
    acceptance_transform,
    lookup_transform,
    payload_transform,
    gating_transform,
    fading_baseline,
    fading_left_factor,
    fading_right_factor,
    present_reward,
    group_layer_scaling,
    group_layer_shift_term,
    final_transform,
):
    long_rows = continued_prompt_entries.shape[0]
    requests = prompt_live_extents.shape[0]
    slot_rows = padded_prompt_entries.shape[0] // requests
    per_group_view, embedding_dimension = present_reward.shape
    seq_count = lax.axis_size("z") * lax.axis_size("core")
    arrived = seq_shift(continued_prompt_entries[-1:], 1, seq_count)
    first = seq_index() == 0
    edge_row = jnp.where(first, preceding_entry_line[None, :], arrived)
    stacked = jnp.concatenate([continued_prompt_entries, padded_prompt_entries, edge_row], axis=0)
    stacked = lax.all_gather(stacked, "mp", axis=1, tiled=True)
    current = stacked[: long_rows + padded_prompt_entries.shape[0]]
    edge_full = stacked[-1:]
    previous = shifted_rows(current, edge_full, long_rows, requests, slot_rows)
    mixes = [mix_rows(current, previous, token_mixing_ratios[index]) for index in range(5)]
    total_rows = current.shape[0]
    columns = acceptance_transform.shape[1]
    blocks = jnp.stack(
        [
            acceptance_transform,
            lookup_transform,
            payload_transform,
            gating_transform,
            final_transform.T,
        ],
        axis=0,
    )
    blocks = lax.all_gather(lax.all_gather(blocks, "z"), "core")
    cores, chips, kinds, depth, width = blocks.shape
    blocks = jnp.transpose(blocks, (2, 1, 0, 3, 4)).reshape(kinds, chips * cores * depth, width)
    pieces = tuple((blocks[index] for index in range(4)))
    acceptance_entries, lookup_entries, payload_entries, gate = tuple(
        (
            jnp.dot(source, piece, preferred_element_type=jnp.float32)
            for source, piece in zip(mixes[:4], pieces)
        )
    )
    squeezed = jnp.tanh(
        jnp.dot(mixes[4], fading_left_factor, preferred_element_type=jnp.float32)
    ).astype(jnp.bfloat16)
    log_fading_amount = -jnp.exp(
        fading_baseline[None, :]
        + jnp.dot(squeezed, fading_right_factor, preferred_element_type=jnp.float32)
    )
    recept3, keys3, values3, decay3 = [
        a.reshape(total_rows, per_group_view, embedding_dimension)
        for a in (acceptance_entries, lookup_entries, payload_entries, log_fading_amount)
    ]
    local_state, long_out = continued_recurrence(
        recept3[:long_rows],
        keys3[:long_rows],
        values3[:long_rows],
        decay3[:long_rows],
        present_reward,
    )
    long_decay = decay3[:long_rows]
    group_total = jnp.sum(long_decay, axis=0)
    start = (jnp.zeros((per_group_view, embedding_dimension), jnp.float32), carried_memory)
    _, incoming = exclusive_prefix((group_total, local_state), start, seq_count)
    before_row = jnp.cumsum(long_decay, axis=0) - long_decay
    long_out = long_out + jnp.einsum(
        "ihc,hcd->ihd", recept3[:long_rows] * jnp.exp(before_row), incoming, precision=highest
    )
    span_end = jnp.exp(group_total)[:, :, None] * incoming + local_state
    live_rows = (
        lax.broadcasted_iota(jnp.int32, (requests, slot_rows), 1) < prompt_live_extents[:, None]
    )
    live_flat = live_rows.reshape(requests * slot_rows).astype(jnp.float32)[:, None, None]
    short_shape = (requests, slot_rows, per_group_view, embedding_dimension)
    short_recept = recept3[long_rows:].reshape(short_shape)
    short_keys = (keys3[long_rows:] * live_flat).reshape(short_shape)
    short_values = values3[long_rows:].reshape(short_shape)
    short_decay = (decay3[long_rows:] * live_flat).reshape(short_shape)
    zeroed_memory = jnp.zeros(
        (per_group_view, embedding_dimension, embedding_dimension), jnp.float32
    )

    def request_pass(acceptance_lines, lookup_table, payload_table, fading_table):
        return block_sweep(
            zeroed_memory,
            acceptance_lines,
            lookup_table,
            payload_table,
            fading_table,
            present_reward,
        )

    request_states, short_out = jax.vmap(request_pass)(
        short_recept, short_keys, short_values, short_decay
    )
    wkv = jnp.concatenate(
        [long_out, short_out.reshape(requests * slot_rows, per_group_view, embedding_dimension)],
        axis=0,
    )
    mean = jnp.mean(wkv, axis=-1, keepdims=True)
    centred = wkv - mean
    variance = jnp.mean(centred * centred, axis=-1, keepdims=True)
    normed = (centred * lax.rsqrt(variance + norm_eps)).reshape(
        total_rows, columns
    ) * group_layer_scaling[None, :] + group_layer_shift_term[None, :]
    row_live = jnp.concatenate(
        [jnp.ones((long_rows,), dtype=bool), live_rows.reshape(requests * slot_rows)], axis=0
    )
    hidden = jnp.where(row_live[:, None], normed * jax.nn.silu(gate), 0.0).astype(jnp.bfloat16)
    full_out = blocks[4]
    mixed_rows = lax.psum_scatter(
        lax.dot_general(
            hidden, full_out, (((1,), (1,)), ((), ())), preferred_element_type=jnp.float32
        ),
        "mp",
        scatter_dimension=0,
        tiled=True,
    )
    return (mixed_rows.astype(jnp.bfloat16)[None], span_end[None], request_states)


def solution(mesh):
    placed = (
        P("seq", "mp"),
        P("seq", "mp"),
        P("seq"),
        P("mp"),
        P("mp", None, None),
        P(),
        P("seq", "mp"),
        P("seq", "mp"),
        P("seq", "mp"),
        P("seq", "mp"),
        P("mp"),
        P(),
        P(None, "mp"),
        P("mp", None),
        P("mp"),
        P("mp"),
        P("mp", "seq"),
    )
    devices = mesh.devices
    seq_devices, mp_devices = devices.shape
    mesh = jax.sharding.Mesh(devices.reshape(seq_devices // 2, 2, mp_devices), ("z", "core", "mp"))
    placed = tuple((P(*[SEQ if name == "seq" else name for name in spec]) for spec in placed))
    return jax.shard_map(
        on_device,
        mesh=mesh,
        in_specs=placed,
        out_specs=(P(SEQ, "mp", None), P(SEQ, "mp", None, None), P(SEQ, "mp", None, None)),
        check_vma=False,
    )
```

profile of v0, /device:TPU:2, one launch (start us, length us, event | category | flops | bytes accessed | tf_op | source)
XLA Modules:
  0.0 407.3 jit_solution(4726152788664702614)
XLA Ops:
  13.1 1.7 collective-permute-start
  17.9 80.3 %all-gather.8.cloned.1.call-done = bf16[80,128,256]{2,1,0:T(8,128)(2,1)} async-done(((bf16[5,128,256]{2,1,0:T(8,128)(2,1)}), bf16[80,128,256]{2,1,0:T(8,128)(2,1)}) %all-gather.8.cloned.1.call-update) | async-done | bytes 5242896 | tf_op jit(solution)/shard_map/all_gather | solution.py:164
  99.8 60.9 %all-gather.6.cloned.1.call-done = bf16[257,4096]{1,0:T(8,128)(2,1)} async-done(((bf16[257,256]{1,0:T(8,128)(2,1)}), bf16[257,4096]{1,0:T(8,128)(2,1)}) %all-gather.6.cloned.1.call-update) | async-done | bytes 2105360 | tf_op jit(solution)/shard_map/all_gather | solution.py:147
  160.7 1.9 slice-done
  164.0 3.0 fusion.40
  169.3 4.1 %collective-permute-start.2 = (f32[4,64]{1,0:T(4,128)S(1)}, f32[4,64]{1,0:T(4,128)S(1)}, u32[]{:S(2)}, u32[]{:S(2)}) collective-permute-start(f32[4,64]{1,0:T(4,128)S(1)} %get-tuple-element.130), channel_id=1, source_target_pairs={{0,16},{16,32},{32,48},{48,64},{64,80},{80,96},{96,112},{112,128},... | collective-permute-start | bytes 3080 | tf_op jit(solution)/shard_map/ppermute | solution.py:18
  174.4 6.0 %collective-permute-start.3 = (f32[4,64]{1,0:T(4,128)S(1)}, f32[4,64]{1,0:T(4,128)S(1)}, u32[]{:S(2)}, u32[]{:S(2)}) collective-permute-start(f32[4,64]{1,0:T(4,128)S(1)} %get-tuple-element.128), channel_id=1, source_target_pairs={{0,32},{16,48},{32,64},{48,80},{64,96},{80,112},{96,128},{112,144}... | collective-permute-start | bytes 3080 | tf_op jit(solution)/shard_map/ppermute | solution.py:18
  181.8 5.2 %collective-permute-start.4 = (f32[4,64]{1,0:T(4,128)S(1)}, f32[4,64]{1,0:T(4,128)S(1)}, u32[]{:S(2)}, u32[]{:S(2)}) collective-permute-start(f32[4,64]{1,0:T(4,128)S(1)} %get-tuple-element.126), channel_id=1, source_target_pairs={{0,64},{16,80},{32,96},{48,112},{64,128},{80,144},{96,160},{112,17... | collective-permute-start | bytes 3080 | tf_op jit(solution)/shard_map/ppermute | solution.py:18
  188.2 13.1 %collective-permute-start.5 = (f32[4,64]{1,0:T(4,128)S(1)}, f32[4,64]{1,0:T(4,128)S(1)}, u32[]{:S(2)}, u32[]{:S(2)}) collective-permute-start(f32[4,64]{1,0:T(4,128)S(1)} %get-tuple-element.124), channel_id=1, source_target_pairs={{0,128},{16,144},{32,160},{48,176},{64,192},{80,208},{96,224},{112... | collective-permute-start | bytes 3080 | tf_op jit(solution)/shard_map/ppermute | solution.py:18
  201.4 6.2 %fusion.92 = (bf16[1,16,2,128,256]{4,3,0,1,2:T(8,128)(2,1)}, bf16[1,16,2,128,256]{4,3,0,1,2:T(8,128)(2,1)}, bf16[1,16,2,128,256]{4,3,0,1,2:T(8,128)(2,1)S(1)}, b...) fusion(bf16[5,16,2,128,256]{4,3,0,1,2:T(8,128)(2,1)} %bitcast.142), kind=kLoop, calls=%fused_computation.139 | loop fusion | bytes 20971520 | tf_op jit(solution)/shard_map/slice | solution.py:167
  217.1 13.2 %while.13 = (s32[]{:T(128)}, f32[4,64,64]{2,1,0:T(8,128)S(1)}, f32[2,64,4,64]{1,0,3,2:T(2,128)}, f32[2,64,4,64]{1,0,3,2:T(2,128)S(1)}, f32[2,64,4,64]{3,2,1,0:T(...) while((s32[]{:T(128)}, f32[4,64,64]{2,1,0:T(8,128)S(1)}, ...), condition=%wide.region_3.4_spmd.clone, body=%wide.region_0.3_spmd.clone.sunk | while | flops 51646208 | bytes 2444424 | solution.py:96
  219.4 4.3 %dynamic_update_slice.6 = f32[2,64,4,64]{1,0,3,2:T(2,128)} dynamic-update-slice(f32[2,64,4,64]{1,0,3,2:T(2,128)} %get-tuple-element.235, f32[1,64,4,64]{1,0,3,2:T(1,128)S(1)} %copy.218, s32[]{:T(128)S(6)} %copy.227, s32[]{:T(128)} %constant.28.clone.1..sunk, s32[]{:T(128)} %constant.28.clone.1..sunk, s32[]{:T(128)} %constant.28.clone.1..sunk) | dynamic-update-slice | bytes 131076 | tf_op jit(solution)/shard_map/while/body/jit(dynamic_update_index_in_dim)/dynamic_update_slice | solution.py:96
  226.1 4.3 %dynamic_update_slice.6 = f32[2,64,4,64]{1,0,3,2:T(2,128)} dynamic-update-slice(f32[2,64,4,64]{1,0,3,2:T(2,128)} %get-tuple-element.235, f32[1,64,4,64]{1,0,3,2:T(1,128)S(1)} %copy.218, s32[]{:T(128)S(6)} %copy.227, s32[]{:T(128)} %constant.28.clone.1..sunk, s32[]{:T(128)} %constant.28.clone.1..sunk, s32[]{:T(128)} %constant.28.clone.1..sunk) | dynamic-update-slice | bytes 131076 | tf_op jit(solution)/shard_map/while/body/jit(dynamic_update_index_in_dim)/dynamic_update_slice | solution.py:96
  236.5 2.1 exponential_multiply_fusion
  238.6 5.3 %collective-permute-start.8 = (f32[4,64,64]{2,1,0:T(8,128)S(1)}, f32[4,64,64]{2,1,0:T(8,128)S(1)}, u32[]{:S(2)}, u32[]{:S(2)}) collective-permute-start(f32[4,64,64]{2,1,0:T(8,128)S(1)} %add_select_fusion.4), channel_id=1, source_target_pairs={{0,32},{16,48},{32,64},{48,80},{64,96},{80,112},{96,128},{112,144}... | collective-permute-start | bytes 196616 | tf_op jit(solution)/shard_map/ppermute | solution.py:18
  244.9 2.5 collective-permute-done.8
  247.5 6.3 %collective-permute-start.9 = (f32[4,64,64]{2,1,0:T(8,128)S(1)}, f32[4,64,64]{2,1,0:T(8,128)S(1)}, u32[]{:S(2)}, u32[]{:S(2)}) collective-permute-start(f32[4,64,64]{2,1,0:T(8,128)S(1)} %add_select_fusion.3), channel_id=1, source_target_pairs={{0,64},{16,80},{32,96},{48,112},{64,128},{80,144},{96,160},{112,17... | collective-permute-start | bytes 196616 | tf_op jit(solution)/shard_map/ppermute | solution.py:18
  254.4 3.2 collective-permute-done.9
  257.7 12.6 %collective-permute-start.10 = (f32[4,64,64]{2,1,0:T(8,128)S(1)}, f32[4,64,64]{2,1,0:T(8,128)S(1)}, u32[]{:S(2)}, u32[]{:S(2)}) collective-permute-start(f32[4,64,64]{2,1,0:T(8,128)S(1)} %add_select_fusion.2), channel_id=1, source_target_pairs={{0,128},{16,144},{32,160},{48,176},{64,192},{80,208},{96,224},{112... | collective-permute-start | bytes 196616 | tf_op jit(solution)/shard_map/ppermute | solution.py:18
  273.0 13.9 %collective-permute-start.11 = (f32[4,64,64]{2,1,0:T(8,128)S(1)}, f32[4,64,64]{2,1,0:T(8,128)}, u32[]{:S(2)}, u32[]{:S(2)}) collective-permute-start(f32[4,64,64]{2,1,0:T(8,128)S(1)} %add_select_fusion.1), channel_id=1, source_target_pairs={{0,256},{16,272},{32,288},{48,304},{64,320},{80,336},{96,352},{112... | collective-permute-start | bytes 196616 | tf_op jit(solution)/shard_map/ppermute | solution.py:18
  289.5 3.3 copy.156
  292.8 1.8 reshape.151
  294.6 1.8 reshape.148
  296.4 1.8 concatenate.27
  298.2 1.5 copy.155
  299.8 1.8 fusion.41
  302.4 1.8 copy.154
  304.9 1.8 copy.153
  307.5 7.5 %fusion.68 = f32[256,4096]{1,0:T(8,128)} fusion(bf16[4096,256]{1,0:T(8,128)(2,1)} %bitcast.145, f32[256,256]{1,0:T(8,128)} %copy.154, f32[256,256]{1,0:T(8,128)} %copy.153, f32[128,256]{1,0:T(8,128)} %concatenate.27, f32[128,256]{1,0:T(8,128)} %copy.151, bf16[4096,256]{1,0:T(8,128)(2,1)} %bitcast.146, f32[4096]{0:T(1024)S(1)} %bitcast.160, ...), kind=kOutput, calls=%fused_computation.84 | convolution fusion | flops 1086062592 | bytes 13396480 | tf_op jit(solution)/shard_map/dot_general | solution.py:243
  317.3 1.7 add_bitcast_fusion
  319.0 80.1 %reduce-scatter.2.cloned.1.call-done = f32[16,4096]{1,0:T(8,128)} async-done(((f32[256,4096]{1,0:T(8,128)}), f32[16,4096]{1,0:T(8,128)}) %reduce-scatter.2.cloned.1.call-update) | async-done | bytes 262160 | tf_op jit(solution)/shard_map/reduce_scatter | solution.py:242
  399.1 1.6 convert_bitcast_fusion
  (191 shorter events, 49.2 us)
Async XLA Ops:
  7.2 156.8 %copy-start = (bf16[4096,128]{1,0:T(8,128)(2,1)S(1)}, bf16[4096,128]{1,0:T(8,128)(2,1)}, u32[]{:S(2)}) copy-start(bf16[4096,128]{1,0:T(8,128)(2,1)} %param.30) | copy-start | bytes 3145732
  7.2 91.1 %all-gather.8.cloned.1.call-start = ((), (), s32[]{:S(2)}) async-start(), calls=%async_computation.3 | async-start | bytes 5570560 | tf_op jit(solution)/shard_map/all_gather | solution.py:164
  12.4 148.3 %all-gather.6.cloned.1.call-start = ((), (), s32[]{:S(2)}) async-start(), calls=%async_computation.1 | async-start | bytes 2297856 | tf_op jit(solution)/shard_map/all_gather | solution.py:147
  13.1 2.5 collective-permute-start
  17.9 183.5 %all-gather.10.cloned.1.call-start = ((), (), s32[]{:S(2)}) async-start(), calls=%async_computation.4 | async-start | bytes 15728640 | tf_op jit(solution)/shard_map/all_gather | solution.py:164
  98.3 300.9 %reduce-scatter.2.cloned.1.call-start = ((), (), s32[]{:S(2)}) async-start(), calls=%async_computation.2 | async-start | bytes 4456448 | tf_op jit(solution)/shard_map/reduce_scatter | solution.py:242
  162.9 4.1 %copy-start.13 = (bf16[2,64,4096]{2,1,0:T(8,128)(2,1)}, bf16[2,64,4096]{2,1,0:T(8,128)(2,1)S(1)}, u32[]{:S(2)}) copy-start(bf16[2,64,4096]{2,1,0:T(8,128)(2,1)S(1)} %concatenate.24) | copy-start | bytes 3145732
  163.0 4.0 copy-start.27
  164.0 4.5 %copy-start.29 = (s32[2]{0:T(128)S(1)}, s32[2]{0:T(128)}, u32[]{:S(2)}) copy-start(s32[2]{0:T(128)} %param.21) | copy-start | bytes 28
  167.2 2.1 collective-permute-start.1
  169.3 5.1 %collective-permute-start.2 = (f32[4,64]{1,0:T(4,128)S(1)}, f32[4,64]{1,0:T(4,128)S(1)}, u32[]{:S(2)}, u32[]{:S(2)}) collective-permute-start(f32[4,64]{1,0:T(4,128)S(1)} %get-tuple-element.130), channel_id=1, source_target_pairs={{0,16},{16,32},{32,48},{48,64},{64,80},{80,96},{96,112},{112,128},... | collective-permute-start | bytes 3080 | tf_op jit(solution)/shard_map/ppermute | solution.py:18
  174.4 33.2 %copy-start.7 = (f32[2,64,4,64]{3,2,1,0:T(4,128)}, f32[2,64,4,64]{3,2,1,0:T(4,128)S(1)}, u32[]{:S(2)}) copy-start(f32[2,64,4,64]{3,2,1,0:T(4,128)S(1)} %copy.141) | copy-start | bytes 393220
  174.4 7.3 %collective-permute-start.3 = (f32[4,64]{1,0:T(4,128)S(1)}, f32[4,64]{1,0:T(4,128)S(1)}, u32[]{:S(2)}, u32[]{:S(2)}) collective-permute-start(f32[4,64]{1,0:T(4,128)S(1)} %get-tuple-element.128), channel_id=1, source_target_pairs={{0,32},{16,48},{32,64},{48,80},{64,96},{80,112},{96,128},{112,144}... | collective-permute-start | bytes 3080 | tf_op jit(solution)/shard_map/ppermute | solution.py:18
  180.7 6.3 %copy-start.12 = (f32[2,64,4,64]{3,2,1,0:T(4,128)}, f32[2,64,4,64]{3,2,1,0:T(4,128)S(1)}, u32[]{:S(2)}) copy-start(f32[2,64,4,64]{3,2,1,0:T(4,128)S(1)} %fusion.72) | copy-start | bytes 393220
  181.8 6.5 %collective-permute-start.4 = (f32[4,64]{1,0:T(4,128)S(1)}, f32[4,64]{1,0:T(4,128)S(1)}, u32[]{:S(2)}, u32[]{:S(2)}) collective-permute-start(f32[4,64]{1,0:T(4,128)S(1)} %get-tuple-element.126), channel_id=1, source_target_pairs={{0,64},{16,80},{32,96},{48,112},{64,128},{80,144},{96,160},{112,17... | collective-permute-start | bytes 3080 | tf_op jit(solution)/shard_map/ppermute | solution.py:18
  188.2 43.4 %collective-permute-start.5 = (f32[4,64]{1,0:T(4,128)S(1)}, f32[4,64]{1,0:T(4,128)S(1)}, u32[]{:S(2)}, u32[]{:S(2)}) collective-permute-start(f32[4,64]{1,0:T(4,128)S(1)} %get-tuple-element.124), channel_id=1, source_target_pairs={{0,128},{16,144},{32,160},{48,176},{64,192},{80,208},{96,224},{112... | collective-permute-start | bytes 3080 | tf_op jit(solution)/shard_map/ppermute | solution.py:18
  201.4 6.4 %copy-start.16 = (bf16[127,4096]{1,0:T(8,128)(2,1)S(1)}, bf16[127,4096]{1,0:T(8,128)(2,1)}, u32[]{:S(2)}) copy-start(bf16[127,4096]{1,0:T(8,128)(2,1)} %copy-done.15) | copy-start | bytes 3121156
  230.3 3.7 collective-permute-start.6
  232.7 11.8 %copy-start.19 = (f32[128,256]{1,0:T(8,128)S(1)}, f32[128,256]{1,0:T(8,128)}, u32[]{:S(2)}) copy-start(f32[128,256]{1,0:T(8,128)} %get-tuple-element.152) | copy-start | bytes 393220
  235.0 3.5 collective-permute-start.7
  238.6 8.7 %collective-permute-start.8 = (f32[4,64,64]{2,1,0:T(8,128)S(1)}, f32[4,64,64]{2,1,0:T(8,128)S(1)}, u32[]{:S(2)}, u32[]{:S(2)}) collective-permute-start(f32[4,64,64]{2,1,0:T(8,128)S(1)} %add_select_fusion.4), channel_id=1, source_target_pairs={{0,32},{16,48},{32,64},{48,80},{64,96},{80,112},{96,128},{112,144}... | collective-permute-start | bytes 196616 | tf_op jit(solution)/shard_map/ppermute | solution.py:18
  244.8 43.8 %copy-start.5 = (f32[2,64,4,64]{1,3,2,0:T(8,128)}, f32[2,64,4,64]{1,3,2,0:T(8,128)S(1)}, u32[]{:S(2)}) copy-start(f32[2,64,4,64]{1,3,2,0:T(8,128)S(1)} %copy.145) | copy-start | bytes 393220
  247.5 10.1 %collective-permute-start.9 = (f32[4,64,64]{2,1,0:T(8,128)S(1)}, f32[4,64,64]{2,1,0:T(8,128)S(1)}, u32[]{:S(2)}, u32[]{:S(2)}) collective-permute-start(f32[4,64,64]{2,1,0:T(8,128)S(1)} %add_select_fusion.3), channel_id=1, source_target_pairs={{0,64},{16,80},{32,96},{48,112},{64,128},{80,144},{96,160},{112,17... | collective-permute-start | bytes 196616 | tf_op jit(solution)/shard_map/ppermute | solution.py:18
  257.7 15.1 %collective-permute-start.10 = (f32[4,64,64]{2,1,0:T(8,128)S(1)}, f32[4,64,64]{2,1,0:T(8,128)S(1)}, u32[]{:S(2)}, u32[]{:S(2)}) collective-permute-start(f32[4,64,64]{2,1,0:T(8,128)S(1)} %add_select_fusion.2), channel_id=1, source_target_pairs={{0,128},{16,144},{32,160},{48,176},{64,192},{80,208},{96,224},{112... | collective-permute-start | bytes 196616 | tf_op jit(solution)/shard_map/ppermute | solution.py:18
  273.0 19.8 %copy-start.9 = (f32[4,64,64]{2,1,0:T(8,128)}, f32[4,64,64]{2,1,0:T(8,128)S(1)}, u32[]{:S(2)}) copy-start(f32[4,64,64]{2,1,0:T(8,128)S(1)} %add_select_fusion.1) | copy-start | bytes 196612
  273.0 26.8 %collective-permute-start.11 = (f32[4,64,64]{2,1,0:T(8,128)S(1)}, f32[4,64,64]{2,1,0:T(8,128)}, u32[]{:S(2)}, u32[]{:S(2)}) collective-permute-start(f32[4,64,64]{2,1,0:T(8,128)S(1)} %add_select_fusion.1), channel_id=1, source_target_pairs={{0,256},{16,272},{32,288},{48,304},{64,320},{80,336},{96,352},{112... | collective-permute-start | bytes 196616 | tf_op jit(solution)/shard_map/ppermute | solution.py:18
  289.5 8.7 %copy-start.1 = (bf16[1,16,2,128,256]{4,3,0,1,2:T(8,128)(2,1)S(1)}, bf16[1,16,2,128,256]{4,3,0,1,2:T(8,128)(2,1)}, u32[]{:S(2)}) copy-start(bf16[1,16,2,128,256]{4,3,0,1,2:T(8,128)(2,1)} %get-tuple-element.137) | copy-start | bytes 6291460
  298.2 3.4 copy-start.8
  299.7 7.7 %copy-start.4 = (bf16[257,4096]{1,0:T(8,128)(2,1)S(1)}, bf16[257,4096]{1,0:T(8,128)(2,1)}, u32[]{:S(2)}) copy-start(bf16[257,4096]{1,0:T(8,128)(2,1)} %all-gather.6.cloned.1.call-done) | copy-start | bytes 6316036
  299.7 7.7 %copy-start.30 = (f32[256]{0:T(256)S(1)}, f32[256]{0:T(256)}, u32[]{:S(2)}) copy-start(f32[256]{0:T(256)} %param.34) | copy-start | bytes 3076
  299.7 7.7 %copy-start.31 = (f32[256]{0:T(256)S(1)}, f32[256]{0:T(256)}, u32[]{:S(2)}) copy-start(f32[256]{0:T(256)} %param.33) | copy-start | bytes 3076
  299.7 7.7 %copy-start.32 = (pred[256]{0:T(512)(128)(4,1)S(1)}, pred[256]{0:T(512)(128)(4,1)}, u32[]{:S(2)}) copy-start(pred[256]{0:T(512)(128)(4,1)} %concatenate.22) | copy-start | bytes 772
  (18 other events, 27.1 us)
Sparse Core Ops, SparseCore 0:
  12.5 85.6 all-gather.7
  101.8 58.8 all-gather.5
  162.8 33.1 all-gather.9
  315.1 83.9 reduce-scatter.1
where the time goes:
time: 409 us; the launch traced here: 407 us
  waiting for transfers between devices  232 us (57%)
  starting transfers between devices  72.5 us (18%)
  local copies, waits for them, and re-layouts  54.7 us (13%)
  matrix products  21.7 us (5%)
  between operations  14.5 us (4%)
  other arithmetic  11.6 us (3%)
    all_gather x2, waiting for transfers between devices, on_device(): blocks = lax.all_gather(lax.all_gather(blocks, 'z'), 'core')  80.3 us
    reduce_scatter x1, waiting for transfers between devices, on_device(): lax.psum_scatter(lax.dot_general(hidden, full_out, (((1,), (1,)), ((), ()...  80.1 us
    ppermute x12, starting transfers between devices, seq_shift(): return lax.ppermute(x, SEQ, pairs)  72.3 us
    all_gather x1, waiting for transfers between devices, on_device(): stacked = lax.all_gather(stacked, 'mp', axis=1, tiled=True)  60.9 us
    ppermute x12, waiting for transfers between devices, seq_shift(): return lax.ppermute(x, SEQ, pairs)  10.7 us
    unnamed x71, local copies, waits for them, and re-layouts  10.1 us
    dynamic_update_slice x4, local copies, waits for them, and re-layouts, continued_recurrence(): lax.scan(step, jnp.zeros((per_group_view, embedding_dimension, embedding_...  8.76 us
  transfers between devices with their start and end apart: 16, of which 10 were waited for; matrix products, arithmetic and copies ran while one was open for 14% of the time, Pallas kernels for 0%

commit v1 on v0

--- a/solution.py
+++ b/solution.py
@@ -144,7 +144,10 @@
     first = seq_index() == 0
     edge_row = jnp.where(first, preceding_entry_line[None, :], arrived)
     stacked = jnp.concatenate([continued_prompt_entries, padded_prompt_entries, edge_row], axis=0)
-    stacked = lax.all_gather(stacked, "mp", axis=1, tiled=True)
+    size = lax.axis_size("mp")
+    parts = jnp.stack([stacked for _ in range(size)])
+    parts = lax.all_to_all(parts, "mp", split_axis=0, concat_axis=0)
+    stacked = jnp.concatenate(parts, axis=1)
     current = stacked[: long_rows + padded_prompt_entries.shape[0]]
     edge_full = stacked[-1:]
     previous = shifted_rows(current, edge_full, long_rows, requests, slot_rows)

time: 409 us -> 418 us (1.022)
  waiting for transfers between devices: 232 us -> 202 us
  local copies, waits for them, and re-layouts: 54.7 us -> 78 us
  other arithmetic: 11.6 us -> 33 us
    all_gather x1 -> x0, waiting for transfers between devices: 60.9 us -> none  [on_device(): stacked = lax.all_gather(stacked, 'mp', axis=1, tiled=True)]
    all_to_all x0 -> x1, waiting for transfers between devices: none -> 26 us  [on_device(): parts = lax.all_to_all(parts, 'mp', split_axis=0, concat_axis=0)]
    convert_element_type x0 -> x3, other arithmetic: none -> 15.6 us  [mix_rows(): (here + weight[None, :] * (previous.astype(jnp.float32) - here)).astype(j...]
    ppermute x12, starting transfers between devices: 72.3 us -> 61.2 us  [seq_shift(): return lax.ppermute(x, SEQ, pairs)]
    all_to_all x0 -> x1, starting transfers between devices: none -> 7.24 us  [on_device(): parts = lax.all_to_all(parts, 'mp', split_axis=0, concat_axis=0)]
    all_gather x2, waiting for transfers between devices: 80.3 us -> 85.8 us  [on_device(): blocks = lax.all_gather(lax.all_gather(blocks, 'z'), 'core')]
    ppermute x12, waiting for transfers between devices: 10.7 us -> 5.85 us  [seq_shift(): return lax.ppermute(x, SEQ, pairs)]
    reshape x0 -> x2, local copies, waits for them, and re-layouts: none -> 4.6 us  [the longest x1 2.32 us: shifted_rows(): short_view = current[long_rows:].reshape(requests, slot_rows, feature_part)]
  transfers between devices with their start and end apart: 16 -> 16, of which waited for: 10 -> 7; matrix products, arithmetic and copies ran while one was open for 14% -> 25% of each run, Pallas kernels for 0% -> 0%
where the time goes in v1:
time: 418 us; the launch traced here: 416 us
  waiting for transfers between devices  202 us (48%)
  local copies, waits for them, and re-layouts  78 us (19%)
  starting transfers between devices  68.5 us (16%)
  other arithmetic  33 us (8%)
  matrix products  19.2 us (5%)
  between operations  14.4 us (3%)
    all_gather x2, waiting for transfers between devices, on_device(): blocks = lax.all_gather(lax.all_gather(blocks, 'z'), 'core')  85.8 us
    reduce_scatter x1, waiting for transfers between devices, on_device(): lax.psum_scatter(lax.dot_general(hidden, full_out, (((1,), (1,)), ((), ()...  84.5 us
    ppermute x12, starting transfers between devices, seq_shift(): return lax.ppermute(x, SEQ, pairs)  61.2 us
    all_to_all x1, waiting for transfers between devices, on_device(): parts = lax.all_to_all(parts, 'mp', split_axis=0, concat_axis=0)  26 us
    convert_element_type x3, other arithmetic, mix_rows(): (here + weight[None, :] * (previous.astype(jnp.float32) - here)).astype(j...  15.6 us
    unnamed x72, local copies, waits for them, and re-layouts  13.1 us
    dynamic_update_slice x4, local copies, waits for them, and re-layouts, continued_recurrence(): lax.scan(step, jnp.zeros((per_group_view, embedding_dimension, embedding_...  8.77 us
  transfers between devices with their start and end apart: 16, of which 7 were waited for; matrix products, arithmetic and copies ran while one was open for 25% of the time, Pallas kernels for 0%

profile of v1, /device:TPU:2, one launch (start us, length us, event | category | flops | bytes accessed | tf_op | source)
XLA Modules:
  0.0 415.5 jit_solution(3519379236690200677)
XLA Ops:
  12.4 85.8 %all-gather.5.cloned.1.call-done = bf16[80,128,256]{2,1,0:T(8,128)(2,1)} async-done(((bf16[5,128,256]{2,1,0:T(8,128)(2,1)}), bf16[80,128,256]{2,1,0:T(8,128)(2,1)}) %all-gather.5.cloned.1.call-update) | async-done | bytes 5242896 | tf_op jit(solution)/shard_map/all_gather | solution.py:167
  102.7 7.2 %all-to-all-start = ((bf16[16,257,256]{2,1,0:T(8,128)(2,1)}), bf16[16,257,256]{2,1,0:T(8,128)(2,1)S(1)}, u32[]{:S(2)}, u32[]{:S(2)}) async-start(bf16[16,257,256]{2,1,0:T(8,128)(2,1)} %stack.14), calls=%async_computation | async-start | bytes 4325376 | tf_op jit(solution)/shard_map/all_to_all | solution.py:149
  114.5 26.0 %all-to-all-done = bf16[16,257,256]{2,1,0:T(8,128)(2,1)S(1)} async-done(((bf16[16,257,256]{2,1,0:T(8,128)(2,1)}), bf16[16,257,256]{2,1,0:T(8,128)(2,1)S(1)}, u32[]{:S(2)}, u32[]{:S(2)}) %all-to-all-start) | async-done | bytes 2105376 | tf_op jit(solution)/shard_map/all_to_all | solution.py:149
  140.5 2.8 copy.136
  143.3 2.3 slice.147
  148.2 2.7 copy.137
  150.9 2.3 reshape.204
  156.9 2.7 copy.139
  159.6 2.3 copy.138
  161.8 4.6 %fusion.22 = bf16[256,4096]{0,1:T(8,128)(2,1)} fusion(bf16[128,4096]{0,1:T(8,128)(2,1)} %copy.138, bf16[127,4096]{0,1:T(8,128)(2,1)S(1)} %bitcast.167, bf16[1,4096]{0,1:T(8,128)(2,1)S(1)} %bitcast.168, f32[4096]{0:T(1024)S(1)} %bitcast.189, bf16[257,16,256]{0,2,1:T(8,128)(2,1)} %bitcast.164), kind=kLoop, calls=%fused_computation.44 | loop fusion | flops 11534336 | bytes 6307840 | tf_op jit(solution)/shard_map/convert_element_type | solution.py:36
  166.4 2.6 fusion.26
  169.8 2.9 collective-permute-start.1
  172.7 7.6 %fusion.20 = (bf16[256,16,256]{0,2,1:T(8,128)(2,1)}, bf16[256,16,256]{0,2,1:T(8,128)(2,1)}, bf16[256,16,256]{0,2,1:T(8,128)(2,1)}) fusion(f32[16,256]{1,0:T(8,128)} %mul.267, bf16[257,16,256]{0,2,1:T(8,128)(2,1)} %bitcast.165, bf16[128,16,256]{0,2,1:T(8,128)(2,1)} %copy.139, bf16[127,16,256]{0,2,1:T(8,128)(2,1)S(1)} %slice.146, ...), kind=kLoop, calls=%fused_computation.40 | loop fusion | flops 17825792 | bytes 10534912 | tf_op jit(solution)/shard_map/convert_element_type | solution.py:36
  180.9 2.0 collective-permute-start.2
  183.0 3.4 fusion.17
  186.8 3.0 collective-permute-start.3
  191.1 4.5 %collective-permute-start.4 = (f32[4,64]{1,0:T(4,128)S(1)}, f32[4,64]{1,0:T(4,128)S(1)}, u32[]{:S(2)}, u32[]{:S(2)}) collective-permute-start(f32[4,64]{1,0:T(4,128)S(1)} %get-tuple-element.130), channel_id=1, source_target_pairs={{0,64},{16,80},{32,96},{48,112},{64,128},{80,144},{96,160},{112,17... | collective-permute-start | bytes 3080 | tf_op jit(solution)/shard_map/ppermute | solution.py:18
  198.5 7.3 %collective-permute-start.5 = (f32[4,64]{1,0:T(4,128)S(1)}, f32[4,64]{1,0:T(4,128)S(1)}, u32[]{:S(2)}, u32[]{:S(2)}) collective-permute-start(f32[4,64]{1,0:T(4,128)S(1)} %get-tuple-element.128), channel_id=1, source_target_pairs={{0,128},{16,144},{32,160},{48,176},{64,192},{80,208},{96,224},{112... | collective-permute-start | bytes 3080 | tf_op jit(solution)/shard_map/ppermute | solution.py:18
  205.8 5.8 %fusion.62 = (bf16[1,16,2,128,256]{4,3,0,1,2:T(8,128)(2,1)S(1)}, bf16[1,16,2,128,256]{4,3,0,1,2:T(8,128)(2,1)}, bf16[1,16,2,128,256]{4,3,0,1,2:T(8,128)(2,1)S(1)...) fusion(bf16[5,16,2,128,256]{4,3,0,1,2:T(8,128)(2,1)} %bitcast.169), kind=kLoop, calls=%fused_computation.130 | loop fusion | bytes 20971520 | tf_op jit(solution)/shard_map/slice | solution.py:170
  223.5 18.7 %while.13 = (s32[]{:T(128)}, f32[4,64,64]{2,1,0:T(8,128)S(1)}, f32[2,64,4,64]{1,0,3,2:T(2,128)}, f32[2,64,4,64]{1,0,3,2:T(2,128)S(1)}, f32[2,64,4,64]{3,2,1,0:T(...) while((s32[]{:T(128)}, f32[4,64,64]{2,1,0:T(8,128)S(1)}, ...), condition=%wide.region_3.4_spmd.clone, body=%wide.region_0.3_spmd.clone.sunk | while | flops 51646208 | bytes 2444424 | solution.py:96
  228.6 4.3 %dynamic_update_slice.6 = f32[2,64,4,64]{1,0,3,2:T(2,128)} dynamic-update-slice(f32[2,64,4,64]{1,0,3,2:T(2,128)} %get-tuple-element.238, f32[1,64,4,64]{1,0,3,2:T(1,128)S(1)} %copy.231, s32[]{:T(128)S(6)} %copy.240, s32[]{:T(128)} %constant.28.clone.1..sunk, s32[]{:T(128)} %constant.28.clone.1..sunk, s32[]{:T(128)} %constant.28.clone.1..sunk) | dynamic-update-slice | bytes 131076 | tf_op jit(solution)/shard_map/while/body/jit(dynamic_update_index_in_dim)/dynamic_update_slice | solution.py:96
  238.0 4.3 %dynamic_update_slice.6 = f32[2,64,4,64]{1,0,3,2:T(2,128)} dynamic-update-slice(f32[2,64,4,64]{1,0,3,2:T(2,128)} %get-tuple-element.238, f32[1,64,4,64]{1,0,3,2:T(1,128)S(1)} %copy.231, s32[]{:T(128)S(6)} %copy.240, s32[]{:T(128)} %constant.28.clone.1..sunk, s32[]{:T(128)} %constant.28.clone.1..sunk, s32[]{:T(128)} %constant.28.clone.1..sunk) | dynamic-update-slice | bytes 131076 | tf_op jit(solution)/shard_map/while/body/jit(dynamic_update_index_in_dim)/dynamic_update_slice | solution.py:96
  247.0 2.1 collective-permute-start.7
  249.1 2.1 exponential_multiply_fusion
  251.9 6.7 %collective-permute-start.8 = (f32[4,64,64]{2,1,0:T(8,128)}, f32[4,64,64]{2,1,0:T(8,128)}, u32[]{:S(2)}, u32[]{:S(2)}) collective-permute-start(f32[4,64,64]{2,1,0:T(8,128)} %add_select_fusion.4), channel_id=1, source_target_pairs={{0,32},{16,48},{32,64},{48,80},{64,96},{80,112},{96,128},{112,144}... | collective-permute-start | bytes 196616 | tf_op jit(solution)/shard_map/ppermute | solution.py:18
  263.3 3.4 collective-permute-start.9
  267.2 2.8 collective-permute-done.9
  270.8 12.7 %collective-permute-start.10 = (f32[4,64,64]{2,1,0:T(8,128)}, f32[4,64,64]{2,1,0:T(8,128)}, u32[]{:S(2)}, u32[]{:S(2)}) collective-permute-start(f32[4,64,64]{2,1,0:T(8,128)} %add_select_fusion.2), channel_id=1, source_target_pairs={{0,128},{16,144},{32,160},{48,176},{64,192},{80,208},{96,224},{112... | collective-permute-start | bytes 196616 | tf_op jit(solution)/shard_map/ppermute | solution.py:18
  286.7 13.9 %collective-permute-start.11 = (f32[4,64,64]{2,1,0:T(8,128)S(1)}, f32[4,64,64]{2,1,0:T(8,128)}, u32[]{:S(2)}, u32[]{:S(2)}) collective-permute-start(f32[4,64,64]{2,1,0:T(8,128)S(1)} %add_select_fusion.1), channel_id=1, source_target_pairs={{0,256},{16,272},{32,288},{48,304},{64,320},{80,336},{96,352},{112... | collective-permute-start | bytes 196616 | tf_op jit(solution)/shard_map/ppermute | solution.py:18
  302.5 3.2 copy.168
  311.8 6.6 %fusion.43 = f32[256,4096]{1,0:T(8,128)} fusion(bf16[4096,256]{1,0:T(8,128)(2,1)S(1)} %bitcast.172, f32[256,256]{1,0:T(8,128)S(1)} %copy.166, f32[256,256]{1,0:T(8,128)S(1)} %copy.165, f32[128,256]{1,0:T(8,128)S(1)} %concatenate.37, f32[128,256]{1,0:T(8,128)S(1)} %copy.163, f32[256]{0:T(256)S(1)} %copy-done.30, f32[256]{0:T(256)S(1)} %copy-done.31, ...), kind=kOutput, calls=%fused_computation.87 | convolution fusion | flops 1074528256 | bytes 11274496 | tf_op jit(solution)/shard_map/dot_general | solution.py:246
  322.9 84.5 %reduce-scatter.2.cloned.1.call-done = f32[16,4096]{1,0:T(8,128)} async-done(((f32[256,4096]{1,0:T(8,128)}), f32[16,4096]{1,0:T(8,128)}) %reduce-scatter.2.cloned.1.call-update) | async-done | bytes 262160 | tf_op jit(solution)/shard_map/reduce_scatter | solution.py:245
  (203 shorter events, 76.6 us)
Async XLA Ops:
  7.2 159.3 %copy-start = (bf16[4096,128]{1,0:T(8,128)(2,1)S(1)}, bf16[4096,128]{1,0:T(8,128)(2,1)}, u32[]{:S(2)}) copy-start(bf16[4096,128]{1,0:T(8,128)(2,1)} %param.30) | copy-start | bytes 3145732
  7.2 91.1 %all-gather.5.cloned.1.call-start = ((), (), s32[]{:S(2)}) async-start(), calls=%async_computation.3 | async-start | bytes 5570560 | tf_op jit(solution)/shard_map/all_gather | solution.py:167
  12.4 193.4 %all-gather.7.cloned.1.call-start = ((), (), s32[]{:S(2)}) async-start(), calls=%async_computation.4 | async-start | bytes 15728640 | tf_op jit(solution)/shard_map/all_gather | solution.py:167
  99.1 2.1 collective-permute-start
  102.7 7.3 %copy-start.23 = (f32[5,4096]{1,0:T(8,128)S(1)}, f32[5,4096]{1,0:T(8,128)}, u32[]{:S(2)}) copy-start(f32[5,4096]{1,0:T(8,128)} %param.24) | copy-start | bytes 245764
  102.7 37.8 %all-to-all-start = ((bf16[16,257,256]{2,1,0:T(8,128)(2,1)}), bf16[16,257,256]{2,1,0:T(8,128)(2,1)S(1)}, u32[]{:S(2)}, u32[]{:S(2)}) async-start(bf16[16,257,256]{2,1,0:T(8,128)(2,1)} %stack.14), calls=%async_computation | async-start | bytes 4325376 | tf_op jit(solution)/shard_map/all_to_all | solution.py:149
  109.9 297.5 %reduce-scatter.2.cloned.1.call-start = ((), (), s32[]{:S(2)}) async-start(), calls=%async_computation.2 | async-start | bytes 4456448 | tf_op jit(solution)/shard_map/reduce_scatter | solution.py:245
  169.8 10.5 %copy-start.28 = (f32[4,64]{1,0:T(4,128)}, f32[4,64]{1,0:T(4,128)S(1)}, u32[]{:S(2)}) copy-start(f32[4,64]{1,0:T(4,128)S(1)} %reduce_sum.48) | copy-start | bytes 3076
  169.8 13.1 %copy-start.2 = (bf16[16,257,256]{1,2,0:T(8,128)(2,1)S(1)}, bf16[16,257,256]{1,2,0:T(8,128)(2,1)}, u32[]{:S(2)}) copy-start(bf16[16,257,256]{1,2,0:T(8,128)(2,1)} %copy.136) | copy-start | bytes 6316036
  169.8 13.1 %copy-start.4 = (bf16[128,16,256]{0,2,1:T(8,128)(2,1)S(1)}, bf16[128,16,256]{0,2,1:T(8,128)(2,1)}, u32[]{:S(2)}) copy-start(bf16[128,16,256]{0,2,1:T(8,128)(2,1)} %copy.139) | copy-start | bytes 3145732
  169.8 10.5 %collective-permute-start.1 = (f32[4,64]{1,0:T(4,128)S(1)}, f32[4,64]{1,0:T(4,128)S(1)}, u32[]{:S(2)}, u32[]{:S(2)}) collective-permute-start(f32[4,64]{1,0:T(4,128)S(1)} %reduce_sum.48), channel_id=1, source_target_pairs={{0,16},{16,32},{32,48},{48,64},{64,80},{80,96},{96,112},{112,128},... | collective-permute-start | bytes 3080 | tf_op jit(solution)/shard_map/ppermute | solution.py:18
  180.9 5.5 %copy-start.17 = (f32[128,256]{0,1:T(8,128)S(1)}, f32[128,256]{0,1:T(8,128)}, u32[]{:S(2)}) copy-start(f32[128,256]{0,1:T(8,128)} %get-tuple-element.154) | copy-start | bytes 393220
  180.9 8.9 %copy-start.25 = (f32[2,64]{1,0:T(2,128)S(1)}, f32[2,64]{1,0:T(2,128)}, u32[]{:S(2)}) copy-start(f32[2,64]{1,0:T(2,128)} %get-tuple-element.164) | copy-start | bytes 1540
  180.9 5.9 %collective-permute-start.2 = (f32[4,64]{1,0:T(4,128)S(1)}, f32[4,64]{1,0:T(4,128)S(1)}, u32[]{:S(2)}, u32[]{:S(2)}) collective-permute-start(f32[4,64]{1,0:T(4,128)S(1)} %get-tuple-element.134), channel_id=1, source_target_pairs={{0,16},{16,32},{32,48},{48,64},{64,80},{80,96},{96,112},{112,128},... | collective-permute-start | bytes 3080 | tf_op jit(solution)/shard_map/ppermute | solution.py:18
  186.7 24.9 %copy-start.7 = (f32[2,64,4,64]{3,2,1,0:T(4,128)}, f32[2,64,4,64]{3,2,1,0:T(4,128)S(1)}, u32[]{:S(2)}) copy-start(f32[2,64,4,64]{3,2,1,0:T(4,128)S(1)} %copy.153) | copy-start | bytes 393220
  186.8 4.3 %collective-permute-start.3 = (f32[4,64]{1,0:T(4,128)S(1)}, f32[4,64]{1,0:T(4,128)S(1)}, u32[]{:S(2)}, u32[]{:S(2)}) collective-permute-start(f32[4,64]{1,0:T(4,128)S(1)} %get-tuple-element.132), channel_id=1, source_target_pairs={{0,32},{16,48},{32,64},{48,80},{64,96},{80,112},{96,128},{112,144}... | collective-permute-start | bytes 3080 | tf_op jit(solution)/shard_map/ppermute | solution.py:18
  190.0 21.7 %copy-start.13 = (f32[2,64,4,64]{3,2,1,0:T(4,128)}, f32[2,64,4,64]{3,2,1,0:T(4,128)S(1)}, u32[]{:S(2)}) copy-start(f32[2,64,4,64]{3,2,1,0:T(4,128)S(1)} %fusion.40) | copy-start | bytes 393220
  191.1 7.4 %collective-permute-start.4 = (f32[4,64]{1,0:T(4,128)S(1)}, f32[4,64]{1,0:T(4,128)S(1)}, u32[]{:S(2)}, u32[]{:S(2)}) collective-permute-start(f32[4,64]{1,0:T(4,128)S(1)} %get-tuple-element.130), channel_id=1, source_target_pairs={{0,64},{16,80},{32,96},{48,112},{64,128},{80,144},{96,160},{112,17... | collective-permute-start | bytes 3080 | tf_op jit(solution)/shard_map/ppermute | solution.py:18
  198.5 45.2 %collective-permute-start.5 = (f32[4,64]{1,0:T(4,128)S(1)}, f32[4,64]{1,0:T(4,128)S(1)}, u32[]{:S(2)}, u32[]{:S(2)}) collective-permute-start(f32[4,64]{1,0:T(4,128)S(1)} %get-tuple-element.128), channel_id=1, source_target_pairs={{0,128},{16,144},{32,160},{48,176},{64,192},{80,208},{96,224},{112... | collective-permute-start | bytes 3080 | tf_op jit(solution)/shard_map/ppermute | solution.py:18
  219.3 4.3 %copy-start.20 = (f32[4,64]{1,0:T(4,128)S(1)}, f32[4,64]{1,0:T(4,128)}, u32[]{:S(2)}) copy-start(f32[4,64]{1,0:T(4,128)} %param.32) | copy-start | bytes 3076
  223.5 25.6 %copy-start.26 = (f32[2,64]{1,0:T(2,128)S(1)}, f32[2,64]{1,0:T(2,128)}, u32[]{:S(2)}) copy-start(f32[2,64]{1,0:T(2,128)} %get-tuple-element.164) | copy-start | bytes 1540
  242.3 8.9 %copy-start.27 = (f32[4,64]{1,0:T(4,128)S(1)}, f32[4,64]{1,0:T(4,128)}, u32[]{:S(2)}) copy-start(f32[4,64]{1,0:T(4,128)} %get-tuple-element.133) | copy-start | bytes 3076
  242.3 16.4 %copy-start.24 = (pred[64,64]{1,0:T(8,128)(4,1)S(1)}, pred[64,64]{1,0:T(8,128)(4,1)}, u32[]{:S(2)}) copy-start(pred[64,64]{1,0:T(8,128)(4,1)} %iota_compare_fusion.1) | copy-start | bytes 12292
  242.3 3.8 collective-permute-start.6
  247.0 4.2 %collective-permute-start.7 = (f32[4,64,64]{2,1,0:T(8,128)S(1)}, f32[4,64,64]{2,1,0:T(8,128)S(1)}, u32[]{:S(2)}, u32[]{:S(2)}) collective-permute-start(f32[4,64,64]{2,1,0:T(8,128)S(1)} %broadcast_select_fusion), channel_id=1, source_target_pairs={{0,16},{16,32},{32,48},{48,64},{64,80},{80,96},{96,112},{112,128},... | collective-permute-start | bytes 196616 | tf_op jit(solution)/shard_map/ppermute | solution.py:18
  251.9 10.2 %collective-permute-start.8 = (f32[4,64,64]{2,1,0:T(8,128)}, f32[4,64,64]{2,1,0:T(8,128)}, u32[]{:S(2)}, u32[]{:S(2)}) collective-permute-start(f32[4,64,64]{2,1,0:T(8,128)} %add_select_fusion.4), channel_id=1, source_target_pairs={{0,32},{16,48},{32,64},{48,80},{64,96},{80,112},{96,128},{112,144}... | collective-permute-start | bytes 196616 | tf_op jit(solution)/shard_map/ppermute | solution.py:18
  259.2 41.4 %copy-start.6 = (f32[128,4,64]{2,1,0:T(4,128)S(1)}, f32[128,4,64]{2,1,0:T(4,128)}, u32[]{:S(2)}) copy-start(f32[128,4,64]{2,1,0:T(4,128)} %copy.148) | copy-start | bytes 393220
  263.3 6.8 %collective-permute-start.9 = (f32[4,64,64]{2,1,0:T(8,128)S(1)}, f32[4,64,64]{2,1,0:T(8,128)S(1)}, u32[]{:S(2)}, u32[]{:S(2)}) collective-permute-start(f32[4,64,64]{2,1,0:T(8,128)S(1)} %add_select_fusion.3), channel_id=1, source_target_pairs={{0,64},{16,80},{32,96},{48,112},{64,128},{80,144},{96,160},{112,17... | collective-permute-start | bytes 196616 | tf_op jit(solution)/shard_map/ppermute | solution.py:18
  270.8 14.8 %collective-permute-start.10 = (f32[4,64,64]{2,1,0:T(8,128)}, f32[4,64,64]{2,1,0:T(8,128)}, u32[]{:S(2)}, u32[]{:S(2)}) collective-permute-start(f32[4,64,64]{2,1,0:T(8,128)} %add_select_fusion.2), channel_id=1, source_target_pairs={{0,128},{16,144},{32,160},{48,176},{64,192},{80,208},{96,224},{112... | collective-permute-start | bytes 196616 | tf_op jit(solution)/shard_map/ppermute | solution.py:18
  286.7 22.7 %copy-start.11 = (f32[4,64,64]{2,1,0:T(8,128)}, f32[4,64,64]{2,1,0:T(8,128)S(1)}, u32[]{:S(2)}) copy-start(f32[4,64,64]{2,1,0:T(8,128)S(1)} %add_select_fusion.1) | copy-start | bytes 196612
  286.7 22.7 %collective-permute-start.11 = (f32[4,64,64]{2,1,0:T(8,128)S(1)}, f32[4,64,64]{2,1,0:T(8,128)}, u32[]{:S(2)}, u32[]{:S(2)}) collective-permute-start(f32[4,64,64]{2,1,0:T(8,128)S(1)} %add_select_fusion.1), channel_id=1, source_target_pairs={{0,256},{16,272},{32,288},{48,304},{64,320},{80,336},{96,352},{112... | collective-permute-start | bytes 196616 | tf_op jit(solution)/shard_map/ppermute | solution.py:18
  318.4 90.6 %copy-start.1 = (bf16[4096,128]{1,0:T(8,128)(2,1)S(1)}, bf16[4096,128]{1,0:T(8,128)(2,1)}, u32[]{:S(2)}) copy-start(bf16[4096,128]{1,0:T(8,128)(2,1)} %param.30) | copy-start | bytes 3145732
  (17 other events, 31.6 us)
Sparse Core Ops, SparseCore 0:
  12.5 85.6 all-gather.4
  100.3 29.2 all-gather.6
  318.6 88.7 reduce-scatter.1
